TPU v7x, 128 devices: a whole 4x4x4 slice. The times are simulated.
128 devices in a mesh: node: 4 (over z), wide: 32 (over y, x, core).
Axes of the slice: x: 4, y: 4, z: 4, core: 2. Of those that a mesh axis runs over, the one named last changes fastest.
Arguments:
- tokens: bfloat16 [65536, 768], P(('node', 'wide')), may hold values from -6 to 6
- expert_index: int32 [65536, 1], P(('node', 'wide')), may hold values from 0 to 255; in each aligned block of 512 rows (0 to 511, 512 to 1023, ...) at most 4 rows name the same one
- norm_gain: float32 [768], replicated, may hold values from 0.5 to 1.5
- router_weight: float32 [768, 256], replicated, may hold values from -0.21875 to 0.21875
- expert_in: bfloat16 [256, 768, 3072], P(('node', 'wide')), may hold values from -0.21875 to 0.21875
- expert_out: bfloat16 [256, 3072, 768], P(('node', 'wide')), may hold values from -0.109375 to 0.109375
- post_gain: float32 [768], replicated, may hold values from 0.5 to 1.5
- dense_in: bfloat16 [3072, 768], P('node'), may hold values from -0.21875 to 0.21875
- scale_in: float32 [3072], P('node'), may hold values from 0.5 to 2
- dense_out: bfloat16 [3072, 768], P('node'), may hold values from -0.109375 to 0.109375
- scale_out: float32 [768], replicated, may hold values from 0.5 to 2
Outputs:
- layer_out: bfloat16 [65536, 768], P(('node', 'wide'))
Inputs may be any that keep to these rules, and one draw needn't show every extreme that they name: `expert_index`: in each aligned block of 512 rows (the tokens of one device) no expert is named by more than 4 rows, a bound that some block reaches.
All inputs are finite; a program needn't handle non-finite values.
Results may differ from a plain program's by a relative error of at most 0.01.
Values may be sent and summed in bfloat16 or wider, within the bound.
No kernel may reach another device: no remote copies, remote signals or barrier semaphores. Data moves between devices by JAX's collectives and lax.ppermute only.
A program may use at most 128 MiB of HBM per device.

v0:
```python
import functools

import jax
import jax.numpy as jnp
from jax import lax
from jax.experimental import pallas as pl
from jax.experimental.pallas import tpu as pltpu
from jax.sharding import PartitionSpec as P

AXES = ("node", "wide")
Y_CHIPS, X_CHIPS, CORES = 4, 4, 2
COLORS = 4
FAR = 3
SCALE_ROWS = 8
LANES = 128
SUB = 8
BF16 = jnp.bfloat16
F32 = jnp.float32


def moved(value, nodes, dz=0, dy=0, dx=0, dc=0):
    def place(z, y, x, c):
        return ((z * Y_CHIPS + y) * X_CHIPS + x) * CORES + c

    pairs = [
        (
            place(z, y, x, c),
            place((z + dz) % nodes, (y + dy) % Y_CHIPS, (x + dx) % X_CHIPS, (c + dc) % CORES),
        )
        for z in range(nodes)
        for y in range(Y_CHIPS)
        for x in range(X_CHIPS)
        for c in range(CORES)
    ]
    return lax.ppermute(value, AXES, pairs)


def position():
    wide = lax.axis_index("wide")
    core = wide % CORES
    x_chip = (wide // CORES) % X_CHIPS
    y_chip = wide // (CORES * X_CHIPS)
    return core, ((x_chip + 2 * y_chip) % COLORS, (2 * x_chip + y_chip) % COLORS)


def joined(first, second):
    top = lax.broadcasted_iota(jnp.int32, first.shape, 1) < SUB // 2
    even = jnp.where(top, first, pltpu.roll(second, SUB // 2, 1))
    odd = jnp.where(top, pltpu.roll(first, SUB // 2, 1), second)
    return even, odd


def pack_columns(rows, block, out_ref):
    count = rows.shape[0] // SUB
    first = rows[:, :LANES].reshape(count, SUB, LANES)
    second = rows[:, LANES:].reshape(count, SUB, LANES)
    even, odd = joined(first, second)
    out_ref[:, 0, block * SUB : (block + 1) * SUB, :] = even.astype(out_ref.dtype)
    out_ref[:, 1, block * SUB : (block + 1) * SUB, :] = odd.astype(out_ref.dtype)


def unpack_messages(message_ref, held, rows_ref):
    count = message_ref.shape[0]
    blocks = rows_ref.shape[1] // (2 * LANES)
    for block in range(blocks):
        tile = pl.ds(pl.multiple_of((held * blocks + block) * SUB, SUB), SUB)
        even = message_ref[:, 0, tile, :].astype(F32)
        odd = message_ref[:, 1, tile, :].astype(F32)
        first, second = joined(even, odd)
        start = block * 2 * LANES
        rows_ref[:, start : start + LANES] = first.reshape(count * SUB, LANES).astype(BF16)
        rows_ref[:, start + LANES : start + 2 * LANES] = second.reshape(count * SUB, LANES).astype(BF16)


def half_copy(source, target, held, held_experts, sems):
    tiles = source.shape[2] // held_experts
    part = pl.ds(held * tiles, tiles)
    return pltpu.make_async_copy(source.at[:, :, part, :], target.at[:, :, part, :], sems.at[held])


def both_ways(row):
    count = row.shape[1]
    floats = row.astype(F32)
    turned = jnp.broadcast_to(floats, (LANES, count)).T
    along_rows = jnp.concatenate([turned] * (count // LANES), axis=1)
    return jnp.broadcast_to(floats, (count, count)), along_rows


def normed_rows(floats, gain):
    square_mean = jnp.mean(floats * floats, axis=-1, keepdims=True)
    return (floats * lax.rsqrt(square_mean + 1e-06) * gain).astype(BF16)


def scale_terms(scale):
    high = scale.astype(BF16).astype(F32)
    middle = (scale - high).astype(BF16).astype(F32)
    low = scale - high - middle
    lines = lax.broadcasted_iota(jnp.int32, (SCALE_ROWS, scale.shape[1]), 0)
    terms = jnp.where(lines == 0, high, jnp.where(lines == 1, middle, jnp.where(lines == 2, low, 0.0)))
    return terms.astype(BF16)


def relay_kernel(size, *refs):
    far, (own, right, left, up, down, scales_ref) = refs[:FAR], refs[FAR:]
    for index, source in enumerate(far):
        for part in range(2):
            whole, shared = ((right, left), (up, down))[part], ((up, down), (right, left))[part]
            for which in range(2):
                start = (part * 2 + which) * size
                piece = source[start : start + size, :]
                for out, line in (
                    (own, (index * 2 + part) * 2 + which),
                    (whole[0], index * 2 + which),
                    (whole[1], index * 2 + which),
                    (shared[which], 2 * FAR + index),
                ):
                    out[line * size : (line + 1) * size, :] = piece
        terms = source[4 * size :, :].astype(F32)
        scales_ref[index] = terms[0:1] + terms[1:2] + terms[2:3]


def weave_copies(size, own_in, own_out, arrays, w_in, w_out, sems):
    shard = own_in.shape[0]
    core, colors = position()
    weights = (w_in, w_out)
    copies = [[[] for _ in range(FAR + 1)] for _ in range(2)]
    for which, own in enumerate((own_in, own_out)):
        copies[which][0].append(
            pltpu.make_async_copy(own, weights[which].at[pl.ds(0, shard), :], sems.at[which, 0])
        )

    def copy(array, row, index, part, which, color, swapped):
        line = (colors[part] + color) % COLORS
        line = line * CORES + (core + swapped) % CORES
        start = pl.multiple_of(shard * (index + 1) + part * (shard // 2) + line * size, 16)
        copies[which][index + 1].append(
            pltpu.make_async_copy(
                arrays[array].at[pl.ds(row * size, size), :],
                weights[which].at[pl.ds(start, size), :],
                sems.at[which, index + 1],
            )
        )

    for swapped in range(CORES):
        base = swapped * 5
        for index in range(FAR):
            for which in range(2):
                for part in range(2):
                    copy(base, (index * 2 + part) * 2 + which, index, part, which, 0, swapped)
                for side in range(4):
                    part, color = side // 2, (-1, 1)[side % 2]
                    copy(base + 1 + side, index * 2 + which, index, part, which, color, swapped)
                    if which == side % 2:
                        copy(base + 1 + side, 2 * FAR + index, index, 1 - part, which, 2, swapped)
    return copies


def cut_kernel(size, scale_hbm, in_hbm, out_hbm, cut_ref, scale_ref, sems, scale_sem):
    half = in_hbm.shape[0] // 2
    core, colors = position()
    copies = []
    for part in range(2):
        start = pl.multiple_of(part * half + (colors[part] * CORES + core) * size, 16)
        for which, codes in enumerate((in_hbm, out_hbm)):
            index = part * 2 + which
            held = cut_ref.at[pl.ds(index * size, size), :]
            copies.append(pltpu.make_async_copy(codes.at[pl.ds(start, size), :], held, sems.at[index]))
    scale_copy = pltpu.make_async_copy(scale_hbm, scale_ref, scale_sem.at[0])
    scale_copy.start()
    for copy in copies:
        copy.start()
    scale_copy.wait()
    cut_ref[4 * size :, :] = scale_terms(scale_ref[...].reshape(1, -1))
    for copy in copies:
        copy.wait()


def dispatch_kernel(capacity, token_ref, row_ref, gain_ref, out_hbm, out_ref, sems):
    normed = normed_rows(token_ref[...].astype(F32), gain_ref[...].reshape(1, -1))
    count = token_ref.shape[0]
    row = row_ref[...]
    along, across = both_ways(row)
    source = lax.broadcasted_iota(jnp.int32, (count, count), 0)
    target = lax.broadcasted_iota(jnp.int32, (count, count), 1)
    same = jnp.where((along == across) & (source < target), 1.0, 0.0)
    slot = jnp.sum(same, axis=0, keepdims=True).astype(jnp.int32)
    place = (row >> 1) * capacity + slot
    blocks = normed.shape[1] // (2 * LANES)
    copies = []
    for held in range(2):
        wanted = jnp.where((row & 1) == held, place, -1)
        selected = jnp.where(source == wanted, 1.0, 0.0).astype(BF16)
        for block in range(blocks):
            columns = normed[:, block * 2 * LANES : (block + 1) * 2 * LANES]
            rows = jnp.dot(selected, columns, preferred_element_type=F32)
            pack_columns(rows, held * blocks + block, out_ref)
        copies.append(half_copy(out_ref, out_hbm, held, 2, sems))
        copies[-1].start()
    for copy in copies:
        copy.wait()


def side_kernel(capacity, token_ref, row_ref, gain_ref, router_ref, marks_ref):
    normed = normed_rows(token_ref[...].astype(F32), gain_ref[...].reshape(1, -1)).astype(F32)
    count = token_ref.shape[0]
    along, across = both_ways(row_ref[...])
    logits = jnp.dot(normed, router_ref[...], precision=lax.Precision.HIGHEST, preferred_element_type=F32)
    experts = logits.shape[1]
    columns = lax.broadcasted_iota(jnp.int32, (count, experts), 1).astype(F32)
    picked = jnp.sum(jnp.where(across[:, :experts] == columns, logits, 0.0), axis=1, keepdims=True)
    gate = 1.0 / (1.0 + jnp.exp(-picked))
    rank = lax.broadcasted_iota(jnp.int32, (count, count), 0)
    other = lax.broadcasted_iota(jnp.int32, (count, count), 1)
    same = jnp.where((along == across) & (other < rank), 1.0, 0.0)
    slot = jnp.sum(same, axis=1, keepdims=True).astype(jnp.int32)
    chosen = across[:, :1].astype(jnp.int32)
    place = (chosen >> 1) * capacity + slot
    marks_ref[:, 0:1] = place.astype(F32)
    marks_ref[:, 1:2] = (chosen & 1).astype(F32)
    marks_ref[:, 2:3] = gate


def expert_kernel(
    message,
    in_hbm,
    out_hbm,
    result_hbm,
    result,
    rows,
    hidden,
    w_in,
    w_out,
    first_sems,
    in_sems,
    out_sems,
    result_sems,
):
    held_experts, width, units = in_hbm.shape
    tile, depth = 1024, 2
    steps, blocks = units // tile, width // (2 * LANES)

    def first_copy(step):
        columns = pl.ds(pl.multiple_of(step * tile, tile), tile)
        return pltpu.make_async_copy(
            in_hbm.at[0, :, columns], w_in.at[0, :, columns], first_sems.at[step]
        )

    def in_copy(held):
        return pltpu.make_async_copy(in_hbm.at[held], w_in.at[held], in_sems.at[held])

    def out_copy(held):
        return pltpu.make_async_copy(out_hbm.at[held], w_out.at[held], out_sems.at[held])

    def result_copy(held, block):
        part = pl.ds((held * blocks + block) * SUB, SUB)
        return pltpu.make_async_copy(
            result.at[:, :, part, :], result_hbm.at[:, :, part, :], result_sems.at[held * blocks + block]
        )

    for step in range(depth):
        first_copy(step).start()
    for held in range(held_experts):
        if held == 0:
            unpack_messages(message, held, rows.at[0])

        def enter(step, carry, held=held):
            if held == 0:
                first_copy(step).wait()

                @pl.when(step + depth < steps)
                def _():
                    first_copy(step + depth).start()

                @pl.when(step + depth == steps)
                def _():
                    out_copy(0).start()

            columns = pl.ds(pl.multiple_of(step * tile, tile), tile)
            value = jnp.dot(rows[held], w_in[held, :, columns], preferred_element_type=F32)
            hidden[:, columns] = jnp.maximum(value, 0.0).astype(BF16)
            return carry

        if held > 0:
            in_copy(held).wait()
            out_copy(held).start()
        lax.fori_loop(0, steps, enter, 0)
        out_copy(held).wait()
        if held + 1 < held_experts:
            in_copy(held + 1).start()
            unpack_messages(message, held + 1, rows.at[held + 1])
        for block in range(blocks):
            columns = slice(block * 2 * LANES, (block + 1) * 2 * LANES)
            value = jnp.dot(hidden[...], w_out[held, :, columns], preferred_element_type=F32)
            pack_columns(value, held * blocks + block, result)
            result_copy(held, block).start()
    for held in range(held_experts):
        for block in range(blocks):
            result_copy(held, block).wait()


def tail_kernel(
    size,
    gain_ref,
    scale_ref,
    scale_out_ref,
    far_scale_ref,
    tokens,
    message,
    marks_hbm,
    own_in,
    own_out,
    *refs,
):
    arrays = refs[:-13]
    result_hbm, result_ref, result_sems = refs[-13:-10]
    w_in, w_out, rows, normed2, hidden, total, scales, sems, marks, marks_sem = refs[-10:]
    copies = weave_copies(size, own_in, own_out, arrays, w_in, w_out, sems)
    held_experts = 2
    count, width = tokens.shape
    units = hidden.shape[1]
    shard = own_in.shape[0]
    marks_copy = pltpu.make_async_copy(marks_hbm, marks, marks_sem.at[0])
    marks_copy.start()
    for node in copies[0]:
        for copy in node:
            copy.start()
    total[...] = jnp.zeros_like(total)
    slots = lax.broadcasted_iota(jnp.int32, (count, count), 1).astype(F32)

    def combine(held, carry):
        unpack_messages(message, held, rows)

        @pl.when(held == 0)
        def _():
            marks_copy.wait()

        chosen = (slots == marks[:, 0:1]) & (marks[:, 1:2] == held.astype(F32))
        picked = jnp.where(chosen, 1.0, 0.0).astype(BF16)
        total[...] += jnp.dot(picked, rows[...], preferred_element_type=F32)
        return carry

    lax.fori_loop(0, held_experts, combine, 0)
    residual = (tokens[...].astype(F32) + marks[:, 2:3] * total[...]).astype(BF16)
    rows[...] = residual
    normed2[...] = normed_rows(residual.astype(F32), gain_ref[...].reshape(1, -1))

    scales[:, :shard] = scale_ref[...].reshape(1, -1)
    for index in range(FAR):
        scales[:, (index + 1) * shard : (index + 2) * shard] = far_scale_ref[index]

    def enter(step, carry):
        columns = pl.ds(pl.multiple_of(step * tile, tile), tile)
        value = lax.dot_general(
            normed2[...],
            w_in[columns, :],
            (((1,), (1,)), ((), ())),
            preferred_element_type=F32,
        )
        hidden[:, columns] = jnp.maximum(value * scales[:, columns], 0.0).astype(BF16)
        return carry

    tile = 1024
    bounds = (0, 1, units // tile)
    for part in range(2):
        for node in copies[0][part * (FAR + 1) // 2 : (part + 1) * (FAR + 1) // 2]:
            for copy in node:
                copy.wait()
        if part == 0:
            for node in copies[1]:
                for copy in node:
                    copy.start()
        lax.fori_loop(bounds[part], bounds[part + 1], enter, 0)
    for node in copies[1]:
        for copy in node:
            copy.wait()
    scale_out = scale_out_ref[...].reshape(1, -1)
    tile = 256
    results = []
    for step in range(width // tile):
        columns = slice(step * tile, (step + 1) * tile)
        value = jnp.dot(hidden[...], w_out[:, columns], preferred_element_type=F32)
        value = rows[:, columns].astype(F32) + value * scale_out[:, columns]
        result_ref[:, columns] = value.astype(BF16)
        results.append(
            pltpu.make_async_copy(
                result_ref.at[:, columns], result_hbm.at[:, columns], result_sems.at[step]
            )
        )
        results[-1].start()
    for copy in results:
        copy.wait()


def vmem():
    return pl.BlockSpec(memory_space=pltpu.VMEM)


def hbm():
    return pl.BlockSpec(memory_space=pltpu.HBM)


def call(kernel, out_shape, in_specs, scratch=(), grant=16, out_spec=None, flops=0, moved_bytes=0):
    return pl.pallas_call(
        kernel,
        out_shape=out_shape,
        in_specs=in_specs,
        out_specs=jax.tree.map(lambda _: out_spec or vmem(), out_shape),
        scratch_shapes=list(scratch),
        compiler_params=pltpu.CompilerParams(vmem_limit_bytes=grant << 20),
        cost_estimate=pl.CostEstimate(
            flops=int(flops), bytes_accessed=int(moved_bytes), transcendentals=0
        ),
    )


def stay(value):
    return pltpu.with_memory_space_constraint(value, pltpu.HBM)


def per_device(
    tokens,
    expert_index,
    norm_gain,
    router_weight,
    expert_in,
    expert_out,
    post_gain,
    dense_in,
    scale_in,
    dense_out,
    scale_out,
):
    tok_dev, width = tokens.shape
    experts = router_weight.shape[1]
    held_experts, _, units = expert_in.shape
    devices = experts // held_experts
    capacity = max(2, 2 * tok_dev // experts)
    shard = dense_in.shape[0]
    nodes = units // shard
    size = shard // 2 // (COLORS * CORES)
    message = (devices // 2, 2, held_experts * capacity * width // LANES, LANES)
    like = jax.ShapeDtypeStruct

    row = expert_index.reshape(1, tok_dev)
    dma = pltpu.SemaphoreType.DMA

    cut = call(
        functools.partial(cut_kernel, size),
        like((4 * size + SCALE_ROWS, width), BF16),
        [hbm()] * 3,
        [pltpu.VMEM((shard,), F32), dma((4,)), dma((1,))],
        grant=16,
        moved_bytes=6e5,
    )(stay(scale_in), stay(dense_in), stay(dense_out))
    sent = call(
        functools.partial(dispatch_kernel, capacity),
        like(message, BF16),
        [vmem()] * 3,
        [pltpu.VMEM(message, BF16), dma((held_experts,))],
        out_spec=hbm(),
        flops=4 * tok_dev * tok_dev * width,
        moved_bytes=4e6,
    )(tokens, row, norm_gain)

    far = []
    for step in (1, -1, 2):
        far.append(moved(cut, nodes, dz=step))

    def exchanged(value):
        flat = value.reshape((devices,) + message[2:])
        return lax.all_to_all(flat, AXES, split_axis=0, concat_axis=0, tiled=True).reshape(message)

    arrived = exchanged(sent)

    marks = call(
        functools.partial(side_kernel, capacity),
        like((tok_dev, 3), F32),
        [vmem()] * 4,
        flops=12 * tok_dev * experts * width,
        moved_bytes=4e6,
    )(tokens, row, norm_gain, router_weight)

    side = like((3 * FAR * size, width), BF16)
    own, right, left, up, down, far_scales = call(
        functools.partial(relay_kernel, size),
        [like((4 * FAR * size, width), BF16)] + [side] * 4 + [like((FAR, 1, shard), F32)],
        [vmem()] * FAR,
        moved_bytes=6e6,
    )(*far)
    near = []
    for value, shift in ((right, {"dx": 1}), (left, {"dx": -1}), (up, {"dy": 1}), (down, {"dy": -1})):
        near.append(moved(value, nodes, **shift))
    pieces = [own] + near
    swapped = []
    for value in pieces:
        swapped.append(moved(value, nodes, dc=1))

    rows = devices * capacity
    produced = call(
        expert_kernel,
        like(message, BF16),
        [vmem()] + [hbm()] * 2,
        [
            pltpu.VMEM(message, BF16),
            pltpu.VMEM((held_experts, rows, width), BF16),
            pltpu.VMEM((rows, units), BF16),
            pltpu.VMEM((held_experts, width, units), BF16),
            pltpu.VMEM((held_experts, units, width), BF16),
            dma((units // 1024,)),
            dma((held_experts,)),
            dma((held_experts,)),
            dma((held_experts * width // (2 * LANES),)),
        ],
        grant=40,
        out_spec=hbm(),
        flops=4 * held_experts * rows * units * width,
        moved_bytes=2e7,
    )(arrived, stay(expert_in), stay(expert_out))
    returned = exchanged(produced)

    return call(
        functools.partial(tail_kernel, size),
        like(tokens.shape, BF16),
        [vmem()] * 6 + [hbm()] * 13,
        [
            pltpu.VMEM((tok_dev, width), BF16),
            dma((width // 256,)),
            pltpu.VMEM((units, width), BF16),
            pltpu.VMEM((units, width), BF16),
            pltpu.VMEM((tok_dev, width), BF16),
            pltpu.VMEM((tok_dev, width), BF16),
            pltpu.VMEM((tok_dev, units), BF16),
            pltpu.VMEM((tok_dev, width), F32),
            pltpu.VMEM((1, units), F32),
            dma((2, FAR + 1)),
            pltpu.VMEM((tok_dev, 3), F32),
            dma((1,)),
        ],
        grant=40,
        out_spec=hbm(),
        flops=4 * tok_dev * units * width,
        moved_bytes=1.2e7,
    )(
        post_gain,
        scale_in,
        scale_out,
        far_scales,
        tokens,
        returned,
        *map(stay, [marks, dense_in, dense_out] + pieces + swapped),
    )


def solution(mesh):
    return jax.shard_map(
        per_device,
        mesh=mesh,
        in_specs=(
            P(("node", "wide"), None),
            P(("node", "wide"), None),
            P(),
            P(),
            P(("node", "wide"), None, None),
            P(("node", "wide"), None, None),
            P(),
            P("node", None),
            P("node"),
            P("node", None),
            P(),
        ),
        out_specs=P(("node", "wide"), None),
        check_vma=False,
    )
```

profile of v0, /device:TPU:1, one launch (start us, length us, event | category | flops | bytes accessed | tf_op | source)
XLA Modules:
  0.0 118.3 jit_solution(14286929899387861205)
XLA Ops:
  0.0 1.1 copy-done.3
  1.1 0.7 copy-done.6
  2.5 2.3 %shard_map.111 = bf16[64,2,48,128]{3,2,1,0:T(8,128)(2,1)} custom-call(bf16[512,768]{1,0:T(8,128)(2,1)S(1)} %copy-done.3, s32[1,512]{1,0:T(1,128)S(1)} %bitcast.7, f32[768]{0:T(1024)S(1)} %copy-done.6), custom_call_target="tpu_custom_call" | custom-call | flops 805306368 | bytes 4000000 | tf_op jit(solution)/shard_map/pallas_call | solution.py:455
  4.8 11.5 %all-to-all-start = ((bf16[128,48,128]{2,1,0:T(8,128)(2,1)}), bf16[128,48,128]{2,1,0:T(8,128)(2,1)S(1)}, u32[]{:S(2)}, u32[]{:S(2)}) async-start(bf16[128,48,128]{2,1,0:T(8,128)(2,1)} %bitcast.1), calls=%async_computation | async-start | bytes 3145728 | tf_op jit(solution)/shard_map/all_to_all | solution.py:471
  16.3 1.1 shard_map.109
  17.4 3.3 %collective-permute-start.2 = (bf16[200,768]{1,0:T(8,128)(2,1)S(1)}, bf16[200,768]{1,0:T(8,128)(2,1)S(1)}, u32[]{:S(2)}, u32[]{:S(2)}) collective-permute-start(bf16[200,768]{1,0:T(8,128)(2,1)S(1)} %shard_map.109), channel_id=1, source_target_pairs={{0,64},{1,65},{2,66},{3,67},{4,68},{5,69},{6,70},{7,71},{8,72},{9,... | collective-permute-start | bytes 921608 | tf_op jit(solution)/shard_map/ppermute | solution.py:35
  21.4 0.8 collective-permute-start
  22.2 19.0 %all-to-all-done = bf16[128,48,128]{2,1,0:T(8,128)(2,1)S(1)} async-done(((bf16[128,48,128]{2,1,0:T(8,128)(2,1)}), bf16[128,48,128]{2,1,0:T(8,128)(2,1)S(1)}, u32[]{:S(2)}, u32[]{:S(2)}) %all-to-all-start) | async-done | bytes 1572896 | tf_op jit(solution)/shard_map/all_to_all | solution.py:471
  41.2 14.3 %shard_map.112 = bf16[64,2,48,128]{3,2,1,0:T(8,128)(2,1)} custom-call(bf16[64,2,48,128]{3,2,1,0:T(8,128)(2,1)S(1)} %bitcast.6, bf16[2,768,3072]{2,1,0:T(8,128)(2,1)} %in_hbm.3, bf16[2,3072,768]{2,1,0:T(8,128)(2,1)} %out_hbm.3), custom_call_target="tpu_custom_call" | custom-call | flops 9663676416 | bytes 20000000 | tf_op jit(solution)/shard_map/pallas_call | solution.py:499
  55.5 8.8 %all-to-all-start.1 = ((bf16[128,48,128]{2,1,0:T(8,128)(2,1)}), bf16[128,48,128]{2,1,0:T(8,128)(2,1)S(1)}, u32[]{:S(2)}, u32[]{:S(2)}) async-start(bf16[128,48,128]{2,1,0:T(8,128)(2,1)} %bitcast.3), calls=%async_computation.1 | async-start | bytes 3145728 | tf_op jit(solution)/shard_map/all_to_all | solution.py:471
  64.6 1.4 %collective-permute-start.3 = (bf16[432,768]{1,0:T(8,128)(2,1)S(1)}, bf16[432,768]{1,0:T(8,128)(2,1)S(1)}, u32[]{:S(2)}, u32[]{:S(2)}) collective-permute-start(bf16[432,768]{1,0:T(8,128)(2,1)S(1)} %get-tuple-element.13), channel_id=1, source_target_pairs={{0,2},{1,3},{2,4},{3,5},{4,6},{5,7},{6,0},{7,1},{8,10},{9,11},{10,... | collective-permute-start | bytes 1990664 | tf_op jit(solution)/shard_map/ppermute | solution.py:35
  66.0 1.3 %collective-permute-start.4 = (bf16[432,768]{1,0:T(8,128)(2,1)S(1)}, bf16[432,768]{1,0:T(8,128)(2,1)S(1)}, u32[]{:S(2)}, u32[]{:S(2)}) collective-permute-start(bf16[432,768]{1,0:T(8,128)(2,1)S(1)} %get-tuple-element.14), channel_id=1, source_target_pairs={{0,6},{1,7},{2,0},{3,1},{4,2},{5,3},{6,4},{7,5},{8,14},{9,15},{10,... | collective-permute-start | bytes 1990664 | tf_op jit(solution)/shard_map/ppermute | solution.py:35
  67.4 1.4 %collective-permute-start.5 = (bf16[432,768]{1,0:T(8,128)(2,1)S(1)}, bf16[432,768]{1,0:T(8,128)(2,1)S(1)}, u32[]{:S(2)}, u32[]{:S(2)}) collective-permute-start(bf16[432,768]{1,0:T(8,128)(2,1)S(1)} %get-tuple-element.15), channel_id=1, source_target_pairs={{0,8},{1,9},{2,10},{3,11},{4,12},{5,13},{6,14},{7,15},{8,16},{9,17... | collective-permute-start | bytes 1990664 | tf_op jit(solution)/shard_map/ppermute | solution.py:35
  68.7 1.3 %collective-permute-start.6 = (bf16[432,768]{1,0:T(8,128)(2,1)S(1)}, bf16[432,768]{1,0:T(8,128)(2,1)S(1)}, u32[]{:S(2)}, u32[]{:S(2)}) collective-permute-start(bf16[432,768]{1,0:T(8,128)(2,1)S(1)} %get-tuple-element.16), channel_id=1, source_target_pairs={{0,24},{1,25},{2,26},{3,27},{4,28},{5,29},{6,30},{7,31},{8,0},{9,1... | collective-permute-start | bytes 1990664 | tf_op jit(solution)/shard_map/ppermute | solution.py:35
  70.1 2.2 %collective-permute-start.7 = (bf16[576,768]{1,0:T(8,128)(2,1)S(1)}, bf16[576,768]{1,0:T(8,128)(2,1)S(1)}, u32[]{:S(2)}, u32[]{:S(2)}) collective-permute-start(bf16[576,768]{1,0:T(8,128)(2,1)S(1)} %get-tuple-element.12.refs_0_), channel_id=1, source_target_pairs={{0,1},{1,0},{2,3},{3,2},{4,5},{5,4},{6,7},{7,6},{8,9},{9,8},{10,11... | collective-permute-start | bytes 2654216 | tf_op jit(solution)/shard_map/ppermute | solution.py:35
  72.2 25.8 %collective-permute-done.3.refs_1_ = bf16[432,768]{1,0:T(8,128)(2,1)S(1)} collective-permute-done((bf16[432,768]{1,0:T(8,128)(2,1)S(1)}, bf16[432,768]{1,0:T(8,128)(2,1)S(1)}, u32[]{:S(2)}, u32[]{:S(2)}) %collective-permute-start.3) | collective-permute-done | bytes 663584 | tf_op jit(solution)/shard_map/ppermute | solution.py:35
  98.0 1.0 collective-permute-start.8
  99.8 1.1 copy-done.2
  100.9 1.1 copy-done.4
  102.0 1.8 %shard_map.113.marks_hbm = f32[512,3]{1,0:T(8,128)S(1)} custom-call(bf16[512,768]{1,0:T(8,128)(2,1)S(1)} %copy-done.4, s32[1,512]{1,0:T(1,128)S(1)} %bitcast.8, f32[768]{0:T(1024)S(1)} %copy-done.7, f32[768,256]{1,0:T(8,128)S(1)} %copy-done.2), custom_call_target="tpu_custom_call" | custom-call | flops 1207959552 | bytes 4000000 | tf_op jit(solution)/shard_map/pallas_call | solution.py:475
  103.9 0.7 copy-done.12
  104.7 0.9 copy-done.13
  106.0 0.9 copy-done.20
  106.9 11.2 %shard_map.114 = bf16[512,768]{1,0:T(8,128)(2,1)} custom-call(f32[768]{0:T(1024)S(1)} %copy-done.8, f32[768]{0:T(1024)S(1)} %copy-done, f32[768]{0:T(1024)S(1)} %copy-done.9, f32[3,1,768]{2,1,0:T(1,128)S(1)} %get-tuple-element.11.far_scale_ref, bf16[512,768]{1,0:T(8,128)(2,1)S(1)} %copy-done.5, bf16[64,2,48,128]{3,2,1,0:T(8,128)(2,1)S(1)} %bitcast.5, ...), custom_call_target="tpu_custom_call" | custom-call | flops 4831838208 | bytes 12000000 | tf_op jit(solution)/shard_map/pallas_call | solution.py:521
  (52 shorter events, 2.8 us)
Async XLA Ops:
  4.8 36.4 %all-to-all-start = ((bf16[128,48,128]{2,1,0:T(8,128)(2,1)}), bf16[128,48,128]{2,1,0:T(8,128)(2,1)S(1)}, u32[]{:S(2)}, u32[]{:S(2)}) async-start(bf16[128,48,128]{2,1,0:T(8,128)(2,1)} %bitcast.1), calls=%async_computation | async-start | bytes 3145728 | tf_op jit(solution)/shard_map/all_to_all | solution.py:471
  17.4 46.9 %collective-permute-start.2 = (bf16[200,768]{1,0:T(8,128)(2,1)S(1)}, bf16[200,768]{1,0:T(8,128)(2,1)S(1)}, u32[]{:S(2)}, u32[]{:S(2)}) collective-permute-start(bf16[200,768]{1,0:T(8,128)(2,1)S(1)} %shard_map.109), channel_id=1, source_target_pairs={{0,64},{1,65},{2,66},{3,67},{4,68},{5,69},{6,70},{7,71},{8,72},{9,... | collective-permute-start | bytes 921608 | tf_op jit(solution)/shard_map/ppermute | solution.py:35
  20.8 43.6 %collective-permute-start.1 = (bf16[200,768]{1,0:T(8,128)(2,1)S(1)}, bf16[200,768]{1,0:T(8,128)(2,1)S(1)}, u32[]{:S(2)}, u32[]{:S(2)}) collective-permute-start(bf16[200,768]{1,0:T(8,128)(2,1)S(1)} %shard_map.109), channel_id=1, source_target_pairs={{0,96},{1,97},{2,98},{3,99},{4,100},{5,101},{6,102},{7,103},{8,104... | collective-permute-start | bytes 921608 | tf_op jit(solution)/shard_map/ppermute | solution.py:35
  21.4 43.0 %collective-permute-start = (bf16[200,768]{1,0:T(8,128)(2,1)S(1)}, bf16[200,768]{1,0:T(8,128)(2,1)S(1)}, u32[]{:S(2)}, u32[]{:S(2)}) collective-permute-start(bf16[200,768]{1,0:T(8,128)(2,1)S(1)} %shard_map.109), channel_id=1, source_target_pairs={{0,32},{1,33},{2,34},{3,35},{4,36},{5,37},{6,38},{7,39},{8,40},{9,... | collective-permute-start | bytes 921608 | tf_op jit(solution)/shard_map/ppermute | solution.py:35
  55.5 44.3 %copy-start.7 = (f32[768]{0:T(1024)S(1)}, f32[768]{0:T(1024)}, u32[]{:S(2)}) copy-start(f32[768]{0:T(1024)} %gain_ref.4) | copy-start | bytes 9220
  55.5 44.3 %copy-start.11 = (s32[512,1]{0,1:T(1,128)S(1)}, s32[512,1]{0,1:T(1,128)}, u32[]{:S(2)}) copy-start(s32[512,1]{0,1:T(1,128)} %param.12) | copy-start | bytes 6148
  55.5 51.4 %all-to-all-start.1 = ((bf16[128,48,128]{2,1,0:T(8,128)(2,1)}), bf16[128,48,128]{2,1,0:T(8,128)(2,1)S(1)}, u32[]{:S(2)}, u32[]{:S(2)}) async-start(bf16[128,48,128]{2,1,0:T(8,128)(2,1)} %bitcast.3), calls=%async_computation.1 | async-start | bytes 3145728 | tf_op jit(solution)/shard_map/all_to_all | solution.py:471
  64.6 39.3 %copy-start.1 = (bf16[576,768]{1,0:T(8,128)(2,1)}, bf16[576,768]{1,0:T(8,128)(2,1)S(1)}, u32[]{:S(2)}) copy-start(bf16[576,768]{1,0:T(8,128)(2,1)S(1)} %get-tuple-element.12.refs_0_) | copy-start | bytes 2654212
  64.6 33.4 %collective-permute-start.3 = (bf16[432,768]{1,0:T(8,128)(2,1)S(1)}, bf16[432,768]{1,0:T(8,128)(2,1)S(1)}, u32[]{:S(2)}, u32[]{:S(2)}) collective-permute-start(bf16[432,768]{1,0:T(8,128)(2,1)S(1)} %get-tuple-element.13), channel_id=1, source_target_pairs={{0,2},{1,3},{2,4},{3,5},{4,6},{5,7},{6,0},{7,1},{8,10},{9,11},{10,... | collective-permute-start | bytes 1990664 | tf_op jit(solution)/shard_map/ppermute | solution.py:35
  66.0 32.9 %collective-permute-start.4 = (bf16[432,768]{1,0:T(8,128)(2,1)S(1)}, bf16[432,768]{1,0:T(8,128)(2,1)S(1)}, u32[]{:S(2)}, u32[]{:S(2)}) collective-permute-start(bf16[432,768]{1,0:T(8,128)(2,1)S(1)} %get-tuple-element.14), channel_id=1, source_target_pairs={{0,6},{1,7},{2,0},{3,1},{4,2},{5,3},{6,4},{7,5},{8,14},{9,15},{10,... | collective-permute-start | bytes 1990664 | tf_op jit(solution)/shard_map/ppermute | solution.py:35
  67.4 39.5 %copy-start.8 = (f32[768]{0:T(1024)S(1)}, f32[768]{0:T(1024)}, u32[]{:S(2)}) copy-start(f32[768]{0:T(1024)} %gain_ref.5) | copy-start | bytes 9220
  67.4 31.7 %collective-permute-start.5 = (bf16[432,768]{1,0:T(8,128)(2,1)S(1)}, bf16[432,768]{1,0:T(8,128)(2,1)S(1)}, u32[]{:S(2)}, u32[]{:S(2)}) collective-permute-start(bf16[432,768]{1,0:T(8,128)(2,1)S(1)} %get-tuple-element.15), channel_id=1, source_target_pairs={{0,8},{1,9},{2,10},{3,11},{4,12},{5,13},{6,14},{7,15},{8,16},{9,17... | collective-permute-start | bytes 1990664 | tf_op jit(solution)/shard_map/ppermute | solution.py:35
  68.7 30.8 %collective-permute-start.6 = (bf16[432,768]{1,0:T(8,128)(2,1)S(1)}, bf16[432,768]{1,0:T(8,128)(2,1)S(1)}, u32[]{:S(2)}, u32[]{:S(2)}) collective-permute-start(bf16[432,768]{1,0:T(8,128)(2,1)S(1)} %get-tuple-element.16), channel_id=1, source_target_pairs={{0,24},{1,25},{2,26},{3,27},{4,28},{5,29},{6,30},{7,31},{8,0},{9,1... | collective-permute-start | bytes 1990664 | tf_op jit(solution)/shard_map/ppermute | solution.py:35
  70.0 36.9 %copy-start = (f32[768]{0:T(1024)S(1)}, f32[768]{0:T(1024)}, u32[]{:S(2)}) copy-start(f32[768]{0:T(1024)} %scale_ref.1) | copy-start | bytes 9220
  70.1 34.6 %collective-permute-start.7 = (bf16[576,768]{1,0:T(8,128)(2,1)S(1)}, bf16[576,768]{1,0:T(8,128)(2,1)S(1)}, u32[]{:S(2)}, u32[]{:S(2)}) collective-permute-start(bf16[576,768]{1,0:T(8,128)(2,1)S(1)} %get-tuple-element.12.refs_0_), channel_id=1, source_target_pairs={{0,1},{1,0},{2,3},{3,2},{4,5},{5,4},{6,7},{7,6},{8,9},{9,8},{10,11... | collective-permute-start | bytes 2654216 | tf_op jit(solution)/shard_map/ppermute | solution.py:35
  98.0 5.9 %copy-start.14 = (bf16[432,768]{1,0:T(8,128)(2,1)}, bf16[432,768]{1,0:T(8,128)(2,1)S(1)}, u32[]{:S(2)}) copy-start(bf16[432,768]{1,0:T(8,128)(2,1)S(1)} %collective-permute-done.3.refs_1_) | copy-start | bytes 1990660
  98.0 6.7 %collective-permute-start.8 = (bf16[432,768]{1,0:T(8,128)(2,1)S(1)}, bf16[432,768]{1,0:T(8,128)(2,1)S(1)}, u32[]{:S(2)}, u32[]{:S(2)}) collective-permute-start(bf16[432,768]{1,0:T(8,128)(2,1)S(1)} %collective-permute-done.3.refs_1_), channel_id=1, source_target_pairs={{0,1},{1,0},{2,3},{3,2},{4,5},{5,4},{6,7},{7,6},{8,9},{9,8},{10,11... | collective-permute-start | bytes 1990664 | tf_op jit(solution)/shard_map/ppermute | solution.py:35
  99.0 4.9 %copy-start.15 = (bf16[432,768]{1,0:T(8,128)(2,1)}, bf16[432,768]{1,0:T(8,128)(2,1)S(1)}, u32[]{:S(2)}) copy-start(bf16[432,768]{1,0:T(8,128)(2,1)S(1)} %collective-permute-done.4.refs_2_) | copy-start | bytes 1990660
  99.0 5.7 %collective-permute-start.9 = (bf16[432,768]{1,0:T(8,128)(2,1)S(1)}, bf16[432,768]{1,0:T(8,128)(2,1)S(1)}, u32[]{:S(2)}, u32[]{:S(2)}) collective-permute-start(bf16[432,768]{1,0:T(8,128)(2,1)S(1)} %collective-permute-done.4.refs_2_), channel_id=1, source_target_pairs={{0,1},{1,0},{2,3},{3,2},{4,5},{5,4},{6,7},{7,6},{8,9},{9,8},{10,11... | collective-permute-start | bytes 1990664 | tf_op jit(solution)/shard_map/ppermute | solution.py:35
  99.1 4.9 %copy-start.16 = (bf16[432,768]{1,0:T(8,128)(2,1)}, bf16[432,768]{1,0:T(8,128)(2,1)S(1)}, u32[]{:S(2)}) copy-start(bf16[432,768]{1,0:T(8,128)(2,1)S(1)} %collective-permute-done.5.refs_3_) | copy-start | bytes 1990660
  99.1 5.6 %collective-permute-start.10 = (bf16[432,768]{1,0:T(8,128)(2,1)S(1)}, bf16[432,768]{1,0:T(8,128)(2,1)S(1)}, u32[]{:S(2)}, u32[]{:S(2)}) collective-permute-start(bf16[432,768]{1,0:T(8,128)(2,1)S(1)} %collective-permute-done.5.refs_3_), channel_id=1, source_target_pairs={{0,1},{1,0},{2,3},{3,2},{4,5},{5,4},{6,7},{7,6},{8,9},{9,8},{10,11... | collective-permute-start | bytes 1990664 | tf_op jit(solution)/shard_map/ppermute | solution.py:35
  99.5 7.4 %collective-permute-start.11 = (bf16[432,768]{1,0:T(8,128)(2,1)S(1)}, bf16[432,768]{1,0:T(8,128)(2,1)}, u32[]{:S(2)}, u32[]{:S(2)}) collective-permute-start(bf16[432,768]{1,0:T(8,128)(2,1)S(1)} %collective-permute-done.6.refs_4_), channel_id=1, source_target_pairs={{0,1},{1,0},{2,3},{3,2},{4,5},{5,4},{6,7},{7,6},{8,9},{9,8},{10,11... | collective-permute-start | bytes 1990664 | tf_op jit(solution)/shard_map/ppermute | solution.py:35
  102.0 4.9 %copy-start.5 = (bf16[512,768]{1,0:T(8,128)(2,1)S(1)}, bf16[512,768]{1,0:T(8,128)(2,1)}, u32[]{:S(2)}) copy-start(bf16[512,768]{1,0:T(8,128)(2,1)} %tokens.1) | copy-start | bytes 2359300
  102.0 4.9 %copy-start.9 = (f32[768]{0:T(1024)S(1)}, f32[768]{0:T(1024)}, u32[]{:S(2)}) copy-start(f32[768]{0:T(1024)} %scale_out_ref.1) | copy-start | bytes 9220
  (11 other events, 14.2 us)
where the time goes:
time: 119 us; the launch traced here: 118 us
  waiting for transfers between devices  44.8 us (38%)
  starting transfers between devices  34.5 us (29%)
  Pallas kernels  30.9 us (26%)
  local copies, waits for them, and re-layouts  7.71 us (6%)
    ppermute x12, waiting for transfers between devices, moved(): return lax.ppermute(value, AXES, pairs)  25.8 us
    all_to_all x2, starting transfers between devices, exchanged(): lax.all_to_all(flat, AXES, split_axis=0, concat_axis=0, tiled=True)  20.3 us
    all_to_all x2, waiting for transfers between devices, exchanged(): lax.all_to_all(flat, AXES, split_axis=0, concat_axis=0, tiled=True)  19 us
    pallas_call x1, Pallas kernels, per_device(): call(expert_kernel, like(message, BF16), [vmem()] + [hbm()] * 2, [pltpu.V...  14.3 us
    ppermute x12, starting transfers between devices, moved(): return lax.ppermute(value, AXES, pairs)  14.2 us
    pallas_call x1, Pallas kernels, per_device(): call(functools.partial(tail_kernel, size), like(tokens.shape, BF16), [vme...  11.2 us
    unnamed x42, local copies, waits for them, and re-layouts  7.71 us
  transfers between devices with their start and end apart: 14, of which 2 were waited for; matrix products, arithmetic and copies ran while one was open for 0% of the time, Pallas kernels for 15%

commit v1 on v0

--- a/solution.py
+++ b/solution.py
@@ -245,6 +245,12 @@
             in_hbm.at[0, :, columns], w_in.at[0, :, columns], first_sems.at[step]
         )
 
+    def half_tile_copy(half):
+        columns = pl.ds(pl.multiple_of(half * (tile // 2), tile // 2), tile // 2)
+        return pltpu.make_async_copy(
+            in_hbm.at[0, :, columns], w_in.at[0, :, columns], first_sems.at[half * steps]
+        )
+
     def in_copy(held):
         return pltpu.make_async_copy(in_hbm.at[held], w_in.at[held], in_sems.at[held])
 
@@ -257,7 +263,9 @@
             result.at[:, :, part, :], result_hbm.at[:, :, part, :], result_sems.at[held * blocks + block]
         )
 
-    for step in range(depth):
+    for half in range(2):
+        half_tile_copy(half).start()
+    for step in range(1, depth):
         first_copy(step).start()
     for held in range(held_experts):
         if held == 0:
@@ -280,10 +288,25 @@
             hidden[:, columns] = jnp.maximum(value, 0.0).astype(BF16)
             return carry
 
+        def enter_half(half, carry):
+            half_tile_copy(half).wait()
+
+            @pl.when(half == 0)
+            def _():
+                first_copy(depth).start()
+
+            columns = pl.ds(pl.multiple_of(half * (tile // 2), tile // 2), tile // 2)
+            value = jnp.dot(rows[0], w_in[0, :, columns], preferred_element_type=F32)
+            hidden[:, columns] = jnp.maximum(value, 0.0).astype(BF16)
+            return carry
+
         if held > 0:
             in_copy(held).wait()
             out_copy(held).start()
-        lax.fori_loop(0, steps, enter, 0)
+            lax.fori_loop(0, steps, enter, 0)
+        else:
+            lax.fori_loop(0, 2, enter_half, 0)
+            lax.fori_loop(1, steps, enter, 0)
         out_copy(held).wait()
         if held + 1 < held_experts:
             in_copy(held + 1).start()
@@ -506,7 +529,7 @@
             pltpu.VMEM((rows, units), BF16),
             pltpu.VMEM((held_experts, width, units), BF16),
             pltpu.VMEM((held_experts, units, width), BF16),
-            dma((units // 1024,)),
+            dma((units // 1024 + 1,)),
             dma((held_experts,)),
             dma((held_experts,)),
             dma((held_experts * width // (2 * LANES),)),

time: 119 us -> 119 us (level)
  no operation moved by 1% of the time
where the time goes in v1:
time: 119 us; the launch traced here: 118 us
  waiting for transfers between devices  44.8 us (38%)
  starting transfers between devices  34.5 us (29%)
  Pallas kernels  30.8 us (26%)
  local copies, waits for them, and re-layouts  7.71 us (6%)
    ppermute x12, waiting for transfers between devices, moved(): return lax.ppermute(value, AXES, pairs)  25.8 us
    all_to_all x2, starting transfers between devices, exchanged(): lax.all_to_all(flat, AXES, split_axis=0, concat_axis=0, tiled=True)  20.3 us
    all_to_all x2, waiting for transfers between devices, exchanged(): lax.all_to_all(flat, AXES, split_axis=0, concat_axis=0, tiled=True)  19 us
    pallas_call x1, Pallas kernels, per_device(): call(expert_kernel, like(message, BF16), [vmem()] + [hbm()] * 2, [pltpu.V...  14.2 us
    ppermute x12, starting transfers between devices, moved(): return lax.ppermute(value, AXES, pairs)  14.2 us
    pallas_call x1, Pallas kernels, per_device(): call(functools.partial(tail_kernel, size), like(tokens.shape, BF16), [vme...  11.2 us
    unnamed x42, local copies, waits for them, and re-layouts  7.71 us
  transfers between devices with their start and end apart: 14, of which 2 were waited for; matrix products, arithmetic and copies ran while one was open for 0% of the time, Pallas kernels for 15%

profile of v1, /device:TPU:1, one launch (start us, length us, event | category | flops | bytes accessed | tf_op | source)
XLA Modules:
  0.0 118.2 jit_solution(16343992390271533541)
XLA Ops:
  0.0 1.1 copy-done.3
  1.1 0.7 copy-done.6
  2.5 2.3 %shard_map.111 = bf16[64,2,48,128]{3,2,1,0:T(8,128)(2,1)} custom-call(bf16[512,768]{1,0:T(8,128)(2,1)S(1)} %copy-done.3, s32[1,512]{1,0:T(1,128)S(1)} %bitcast.7, f32[768]{0:T(1024)S(1)} %copy-done.6), custom_call_target="tpu_custom_call" | custom-call | flops 805306368 | bytes 4000000 | tf_op jit(solution)/shard_map/pallas_call | solution.py:478
  4.8 11.5 %all-to-all-start = ((bf16[128,48,128]{2,1,0:T(8,128)(2,1)}), bf16[128,48,128]{2,1,0:T(8,128)(2,1)S(1)}, u32[]{:S(2)}, u32[]{:S(2)}) async-start(bf16[128,48,128]{2,1,0:T(8,128)(2,1)} %bitcast.1), calls=%async_computation | async-start | bytes 3145728 | tf_op jit(solution)/shard_map/all_to_all | solution.py:494
  16.3 1.1 shard_map.109
  17.4 3.3 %collective-permute-start.2 = (bf16[200,768]{1,0:T(8,128)(2,1)S(1)}, bf16[200,768]{1,0:T(8,128)(2,1)S(1)}, u32[]{:S(2)}, u32[]{:S(2)}) collective-permute-start(bf16[200,768]{1,0:T(8,128)(2,1)S(1)} %shard_map.109), channel_id=1, source_target_pairs={{0,64},{1,65},{2,66},{3,67},{4,68},{5,69},{6,70},{7,71},{8,72},{9,... | collective-permute-start | bytes 921608 | tf_op jit(solution)/shard_map/ppermute | solution.py:35
  21.4 0.8 collective-permute-start
  22.2 19.0 %all-to-all-done = bf16[128,48,128]{2,1,0:T(8,128)(2,1)S(1)} async-done(((bf16[128,48,128]{2,1,0:T(8,128)(2,1)}), bf16[128,48,128]{2,1,0:T(8,128)(2,1)S(1)}, u32[]{:S(2)}, u32[]{:S(2)}) %all-to-all-start) | async-done | bytes 1572896 | tf_op jit(solution)/shard_map/all_to_all | solution.py:494
  41.2 14.2 %shard_map.112 = bf16[64,2,48,128]{3,2,1,0:T(8,128)(2,1)} custom-call(bf16[64,2,48,128]{3,2,1,0:T(8,128)(2,1)S(1)} %bitcast.6, bf16[2,768,3072]{2,1,0:T(8,128)(2,1)} %in_hbm.3, bf16[2,3072,768]{2,1,0:T(8,128)(2,1)} %out_hbm.3), custom_call_target="tpu_custom_call" | custom-call | flops 9663676416 | bytes 20000000 | tf_op jit(solution)/shard_map/pallas_call | solution.py:522
  55.4 8.8 %all-to-all-start.1 = ((bf16[128,48,128]{2,1,0:T(8,128)(2,1)}), bf16[128,48,128]{2,1,0:T(8,128)(2,1)S(1)}, u32[]{:S(2)}, u32[]{:S(2)}) async-start(bf16[128,48,128]{2,1,0:T(8,128)(2,1)} %bitcast.3), calls=%async_computation.1 | async-start | bytes 3145728 | tf_op jit(solution)/shard_map/all_to_all | solution.py:494
  64.5 1.4 %collective-permute-start.3 = (bf16[432,768]{1,0:T(8,128)(2,1)S(1)}, bf16[432,768]{1,0:T(8,128)(2,1)S(1)}, u32[]{:S(2)}, u32[]{:S(2)}) collective-permute-start(bf16[432,768]{1,0:T(8,128)(2,1)S(1)} %get-tuple-element.13), channel_id=1, source_target_pairs={{0,2},{1,3},{2,4},{3,5},{4,6},{5,7},{6,0},{7,1},{8,10},{9,11},{10,... | collective-permute-start | bytes 1990664 | tf_op jit(solution)/shard_map/ppermute | solution.py:35
  65.9 1.3 %collective-permute-start.4 = (bf16[432,768]{1,0:T(8,128)(2,1)S(1)}, bf16[432,768]{1,0:T(8,128)(2,1)S(1)}, u32[]{:S(2)}, u32[]{:S(2)}) collective-permute-start(bf16[432,768]{1,0:T(8,128)(2,1)S(1)} %get-tuple-element.14), channel_id=1, source_target_pairs={{0,6},{1,7},{2,0},{3,1},{4,2},{5,3},{6,4},{7,5},{8,14},{9,15},{10,... | collective-permute-start | bytes 1990664 | tf_op jit(solution)/shard_map/ppermute | solution.py:35
  67.3 1.4 %collective-permute-start.5 = (bf16[432,768]{1,0:T(8,128)(2,1)S(1)}, bf16[432,768]{1,0:T(8,128)(2,1)S(1)}, u32[]{:S(2)}, u32[]{:S(2)}) collective-permute-start(bf16[432,768]{1,0:T(8,128)(2,1)S(1)} %get-tuple-element.15), channel_id=1, source_target_pairs={{0,8},{1,9},{2,10},{3,11},{4,12},{5,13},{6,14},{7,15},{8,16},{9,17... | collective-permute-start | bytes 1990664 | tf_op jit(solution)/shard_map/ppermute | solution.py:35
  68.6 1.3 %collective-permute-start.6 = (bf16[432,768]{1,0:T(8,128)(2,1)S(1)}, bf16[432,768]{1,0:T(8,128)(2,1)S(1)}, u32[]{:S(2)}, u32[]{:S(2)}) collective-permute-start(bf16[432,768]{1,0:T(8,128)(2,1)S(1)} %get-tuple-element.16), channel_id=1, source_target_pairs={{0,24},{1,25},{2,26},{3,27},{4,28},{5,29},{6,30},{7,31},{8,0},{9,1... | collective-permute-start | bytes 1990664 | tf_op jit(solution)/shard_map/ppermute | solution.py:35
  70.0 2.2 %collective-permute-start.7 = (bf16[576,768]{1,0:T(8,128)(2,1)S(1)}, bf16[576,768]{1,0:T(8,128)(2,1)S(1)}, u32[]{:S(2)}, u32[]{:S(2)}) collective-permute-start(bf16[576,768]{1,0:T(8,128)(2,1)S(1)} %get-tuple-element.12.refs_0_), channel_id=1, source_target_pairs={{0,1},{1,0},{2,3},{3,2},{4,5},{5,4},{6,7},{7,6},{8,9},{9,8},{10,11... | collective-permute-start | bytes 2654216 | tf_op jit(solution)/shard_map/ppermute | solution.py:35
  72.1 25.8 %collective-permute-done.3.refs_1_ = bf16[432,768]{1,0:T(8,128)(2,1)S(1)} collective-permute-done((bf16[432,768]{1,0:T(8,128)(2,1)S(1)}, bf16[432,768]{1,0:T(8,128)(2,1)S(1)}, u32[]{:S(2)}, u32[]{:S(2)}) %collective-permute-start.3) | collective-permute-done | bytes 663584 | tf_op jit(solution)/shard_map/ppermute | solution.py:35
  97.9 1.0 collective-permute-start.8
  99.7 1.1 copy-done.2
  100.8 1.1 copy-done.4
  101.9 1.8 %shard_map.113.marks_hbm = f32[512,3]{1,0:T(8,128)S(1)} custom-call(bf16[512,768]{1,0:T(8,128)(2,1)S(1)} %copy-done.4, s32[1,512]{1,0:T(1,128)S(1)} %bitcast.8, f32[768]{0:T(1024)S(1)} %copy-done.7, f32[768,256]{1,0:T(8,128)S(1)} %copy-done.2), custom_call_target="tpu_custom_call" | custom-call | flops 1207959552 | bytes 4000000 | tf_op jit(solution)/shard_map/pallas_call | solution.py:498
  103.8 0.7 copy-done.12
  104.6 0.9 copy-done.13
  105.9 0.9 copy-done.20
  106.8 11.2 %shard_map.114 = bf16[512,768]{1,0:T(8,128)(2,1)} custom-call(f32[768]{0:T(1024)S(1)} %copy-done.8, f32[768]{0:T(1024)S(1)} %copy-done, f32[768]{0:T(1024)S(1)} %copy-done.9, f32[3,1,768]{2,1,0:T(1,128)S(1)} %get-tuple-element.11.far_scale_ref, bf16[512,768]{1,0:T(8,128)(2,1)S(1)} %copy-done.5, bf16[64,2,48,128]{3,2,1,0:T(8,128)(2,1)S(1)} %bitcast.5, ...), custom_call_target="tpu_custom_call" | custom-call | flops 4831838208 | bytes 12000000 | tf_op jit(solution)/shard_map/pallas_call | solution.py:544
  (52 shorter events, 2.8 us)
Async XLA Ops:
  4.8 36.4 %all-to-all-start = ((bf16[128,48,128]{2,1,0:T(8,128)(2,1)}), bf16[128,48,128]{2,1,0:T(8,128)(2,1)S(1)}, u32[]{:S(2)}, u32[]{:S(2)}) async-start(bf16[128,48,128]{2,1,0:T(8,128)(2,1)} %bitcast.1), calls=%async_computation | async-start | bytes 3145728 | tf_op jit(solution)/shard_map/all_to_all | solution.py:494
  17.4 46.8 %collective-permute-start.2 = (bf16[200,768]{1,0:T(8,128)(2,1)S(1)}, bf16[200,768]{1,0:T(8,128)(2,1)S(1)}, u32[]{:S(2)}, u32[]{:S(2)}) collective-permute-start(bf16[200,768]{1,0:T(8,128)(2,1)S(1)} %shard_map.109), channel_id=1, source_target_pairs={{0,64},{1,65},{2,66},{3,67},{4,68},{5,69},{6,70},{7,71},{8,72},{9,... | collective-permute-start | bytes 921608 | tf_op jit(solution)/shard_map/ppermute | solution.py:35
  20.8 43.5 %collective-permute-start.1 = (bf16[200,768]{1,0:T(8,128)(2,1)S(1)}, bf16[200,768]{1,0:T(8,128)(2,1)S(1)}, u32[]{:S(2)}, u32[]{:S(2)}) collective-permute-start(bf16[200,768]{1,0:T(8,128)(2,1)S(1)} %shard_map.109), channel_id=1, source_target_pairs={{0,96},{1,97},{2,98},{3,99},{4,100},{5,101},{6,102},{7,103},{8,104... | collective-permute-start | bytes 921608 | tf_op jit(solution)/shard_map/ppermute | solution.py:35
  21.4 42.9 %collective-permute-start = (bf16[200,768]{1,0:T(8,128)(2,1)S(1)}, bf16[200,768]{1,0:T(8,128)(2,1)S(1)}, u32[]{:S(2)}, u32[]{:S(2)}) collective-permute-start(bf16[200,768]{1,0:T(8,128)(2,1)S(1)} %shard_map.109), channel_id=1, source_target_pairs={{0,32},{1,33},{2,34},{3,35},{4,36},{5,37},{6,38},{7,39},{8,40},{9,... | collective-permute-start | bytes 921608 | tf_op jit(solution)/shard_map/ppermute | solution.py:35
  55.4 44.3 %copy-start.7 = (f32[768]{0:T(1024)S(1)}, f32[768]{0:T(1024)}, u32[]{:S(2)}) copy-start(f32[768]{0:T(1024)} %gain_ref.4) | copy-start | bytes 9220
  55.4 44.3 %copy-start.11 = (s32[512,1]{0,1:T(1,128)S(1)}, s32[512,1]{0,1:T(1,128)}, u32[]{:S(2)}) copy-start(s32[512,1]{0,1:T(1,128)} %param.12) | copy-start | bytes 6148
  55.4 51.4 %all-to-all-start.1 = ((bf16[128,48,128]{2,1,0:T(8,128)(2,1)}), bf16[128,48,128]{2,1,0:T(8,128)(2,1)S(1)}, u32[]{:S(2)}, u32[]{:S(2)}) async-start(bf16[128,48,128]{2,1,0:T(8,128)(2,1)} %bitcast.3), calls=%async_computation.1 | async-start | bytes 3145728 | tf_op jit(solution)/shard_map/all_to_all | solution.py:494
  64.5 39.3 %copy-start.1 = (bf16[576,768]{1,0:T(8,128)(2,1)}, bf16[576,768]{1,0:T(8,128)(2,1)S(1)}, u32[]{:S(2)}) copy-start(bf16[576,768]{1,0:T(8,128)(2,1)S(1)} %get-tuple-element.12.refs_0_) | copy-start | bytes 2654212
  64.5 33.4 %collective-permute-start.3 = (bf16[432,768]{1,0:T(8,128)(2,1)S(1)}, bf16[432,768]{1,0:T(8,128)(2,1)S(1)}, u32[]{:S(2)}, u32[]{:S(2)}) collective-permute-start(bf16[432,768]{1,0:T(8,128)(2,1)S(1)} %get-tuple-element.13), channel_id=1, source_target_pairs={{0,2},{1,3},{2,4},{3,5},{4,6},{5,7},{6,0},{7,1},{8,10},{9,11},{10,... | collective-permute-start | bytes 1990664 | tf_op jit(solution)/shard_map/ppermute | solution.py:35
  65.9 32.9 %collective-permute-start.4 = (bf16[432,768]{1,0:T(8,128)(2,1)S(1)}, bf16[432,768]{1,0:T(8,128)(2,1)S(1)}, u32[]{:S(2)}, u32[]{:S(2)}) collective-permute-start(bf16[432,768]{1,0:T(8,128)(2,1)S(1)} %get-tuple-element.14), channel_id=1, source_target_pairs={{0,6},{1,7},{2,0},{3,1},{4,2},{5,3},{6,4},{7,5},{8,14},{9,15},{10,... | collective-permute-start | bytes 1990664 | tf_op jit(solution)/shard_map/ppermute | solution.py:35
  67.3 39.5 %copy-start.8 = (f32[768]{0:T(1024)S(1)}, f32[768]{0:T(1024)}, u32[]{:S(2)}) copy-start(f32[768]{0:T(1024)} %gain_ref.5) | copy-start | bytes 9220
  67.3 31.7 %collective-permute-start.5 = (bf16[432,768]{1,0:T(8,128)(2,1)S(1)}, bf16[432,768]{1,0:T(8,128)(2,1)S(1)}, u32[]{:S(2)}, u32[]{:S(2)}) collective-permute-start(bf16[432,768]{1,0:T(8,128)(2,1)S(1)} %get-tuple-element.15), channel_id=1, source_target_pairs={{0,8},{1,9},{2,10},{3,11},{4,12},{5,13},{6,14},{7,15},{8,16},{9,17... | collective-permute-start | bytes 1990664 | tf_op jit(solution)/shard_map/ppermute | solution.py:35
  68.6 30.8 %collective-permute-start.6 = (bf16[432,768]{1,0:T(8,128)(2,1)S(1)}, bf16[432,768]{1,0:T(8,128)(2,1)S(1)}, u32[]{:S(2)}, u32[]{:S(2)}) collective-permute-start(bf16[432,768]{1,0:T(8,128)(2,1)S(1)} %get-tuple-element.16), channel_id=1, source_target_pairs={{0,24},{1,25},{2,26},{3,27},{4,28},{5,29},{6,30},{7,31},{8,0},{9,1... | collective-permute-start | bytes 1990664 | tf_op jit(solution)/shard_map/ppermute | solution.py:35
  69.9 36.9 %copy-start = (f32[768]{0:T(1024)S(1)}, f32[768]{0:T(1024)}, u32[]{:S(2)}) copy-start(f32[768]{0:T(1024)} %scale_ref.1) | copy-start | bytes 9220
  70.0 34.6 %collective-permute-start.7 = (bf16[576,768]{1,0:T(8,128)(2,1)S(1)}, bf16[576,768]{1,0:T(8,128)(2,1)S(1)}, u32[]{:S(2)}, u32[]{:S(2)}) collective-permute-start(bf16[576,768]{1,0:T(8,128)(2,1)S(1)} %get-tuple-element.12.refs_0_), channel_id=1, source_target_pairs={{0,1},{1,0},{2,3},{3,2},{4,5},{5,4},{6,7},{7,6},{8,9},{9,8},{10,11... | collective-permute-start | bytes 2654216 | tf_op jit(solution)/shard_map/ppermute | solution.py:35
  97.9 5.9 %copy-start.14 = (bf16[432,768]{1,0:T(8,128)(2,1)}, bf16[432,768]{1,0:T(8,128)(2,1)S(1)}, u32[]{:S(2)}) copy-start(bf16[432,768]{1,0:T(8,128)(2,1)S(1)} %collective-permute-done.3.refs_1_) | copy-start | bytes 1990660
  97.9 6.7 %collective-permute-start.8 = (bf16[432,768]{1,0:T(8,128)(2,1)S(1)}, bf16[432,768]{1,0:T(8,128)(2,1)S(1)}, u32[]{:S(2)}, u32[]{:S(2)}) collective-permute-start(bf16[432,768]{1,0:T(8,128)(2,1)S(1)} %collective-permute-done.3.refs_1_), channel_id=1, source_target_pairs={{0,1},{1,0},{2,3},{3,2},{4,5},{5,4},{6,7},{7,6},{8,9},{9,8},{10,11... | collective-permute-start | bytes 1990664 | tf_op jit(solution)/shard_map/ppermute | solution.py:35
  98.9 4.9 %copy-start.15 = (bf16[432,768]{1,0:T(8,128)(2,1)}, bf16[432,768]{1,0:T(8,128)(2,1)S(1)}, u32[]{:S(2)}) copy-start(bf16[432,768]{1,0:T(8,128)(2,1)S(1)} %collective-permute-done.4.refs_2_) | copy-start | bytes 1990660
  98.9 5.7 %collective-permute-start.9 = (bf16[432,768]{1,0:T(8,128)(2,1)S(1)}, bf16[432,768]{1,0:T(8,128)(2,1)S(1)}, u32[]{:S(2)}, u32[]{:S(2)}) collective-permute-start(bf16[432,768]{1,0:T(8,128)(2,1)S(1)} %collective-permute-done.4.refs_2_), channel_id=1, source_target_pairs={{0,1},{1,0},{2,3},{3,2},{4,5},{5,4},{6,7},{7,6},{8,9},{9,8},{10,11... | collective-permute-start | bytes 1990664 | tf_op jit(solution)/shard_map/ppermute | solution.py:35
  99.0 4.9 %copy-start.16 = (bf16[432,768]{1,0:T(8,128)(2,1)}, bf16[432,768]{1,0:T(8,128)(2,1)S(1)}, u32[]{:S(2)}) copy-start(bf16[432,768]{1,0:T(8,128)(2,1)S(1)} %collective-permute-done.5.refs_3_) | copy-start | bytes 1990660
  99.0 5.6 %collective-permute-start.10 = (bf16[432,768]{1,0:T(8,128)(2,1)S(1)}, bf16[432,768]{1,0:T(8,128)(2,1)S(1)}, u32[]{:S(2)}, u32[]{:S(2)}) collective-permute-start(bf16[432,768]{1,0:T(8,128)(2,1)S(1)} %collective-permute-done.5.refs_3_), channel_id=1, source_target_pairs={{0,1},{1,0},{2,3},{3,2},{4,5},{5,4},{6,7},{7,6},{8,9},{9,8},{10,11... | collective-permute-start | bytes 1990664 | tf_op jit(solution)/shard_map/ppermute | solution.py:35
  99.4 7.4 %collective-permute-start.11 = (bf16[432,768]{1,0:T(8,128)(2,1)S(1)}, bf16[432,768]{1,0:T(8,128)(2,1)}, u32[]{:S(2)}, u32[]{:S(2)}) collective-permute-start(bf16[432,768]{1,0:T(8,128)(2,1)S(1)} %collective-permute-done.6.refs_4_), channel_id=1, source_target_pairs={{0,1},{1,0},{2,3},{3,2},{4,5},{5,4},{6,7},{7,6},{8,9},{9,8},{10,11... | collective-permute-start | bytes 1990664 | tf_op jit(solution)/shard_map/ppermute | solution.py:35
  101.9 4.9 %copy-start.5 = (bf16[512,768]{1,0:T(8,128)(2,1)S(1)}, bf16[512,768]{1,0:T(8,128)(2,1)}, u32[]{:S(2)}) copy-start(bf16[512,768]{1,0:T(8,128)(2,1)} %tokens.1) | copy-start | bytes 2359300
  101.9 4.9 %copy-start.9 = (f32[768]{0:T(1024)S(1)}, f32[768]{0:T(1024)}, u32[]{:S(2)}) copy-start(f32[768]{0:T(1024)} %scale_out_ref.1) | copy-start | bytes 9220
  (11 other events, 14.2 us)
